TPU v7x, 32 devices: a whole 2x2x4 slice. The times are simulated.
32 devices in a mesh: narrow: 4 (over y, x), wide: 8 (over z, core).
Axes of the slice: x: 2, y: 2, z: 4, core: 2. Of those that a mesh axis runs over, the one named last changes fastest.
Arguments:
- tokens: bfloat16 [32768, 768], P(('narrow', 'wide')), may hold values from -6 to 6
- frame_counts: int32 [32, 16], P(('narrow', 'wide')), may hold values from 8 to 32, as said below
- segment_ids: int32 [32768], P(('narrow', 'wide')), may hold values from 0 to 13, as said below
- positions: int32 [32768], P(('narrow', 'wide')), may hold values from 0 to 3135, as said below
- cotangent: bfloat16 [32768, 768], P(('narrow', 'wide')), may hold values from -6 to 6
- input_weight: bfloat16 [768, 2304], P('wide'), may hold values from -0.21875 to 0.21875
- output_weight: bfloat16 [768, 768], P('wide'), may hold values from -0.875 to 0.875
- up_weight: bfloat16 [768, 3072], P('wide'), may hold values from -0.21875 to 0.21875
- down_weight: bfloat16 [3072, 768], P('wide'), may hold values from -0.109375 to 0.109375
- pre_gain: bfloat16 [768], P('wide'), may hold values from 0.099609375 to 1.8984375
- pre_bias: bfloat16 [768], P('wide'), may hold values from -3 to 3
- query_bias: bfloat16 [768], P('wide'), may hold values from -3 to 3
- value_bias: bfloat16 [768], P('wide'), may hold values from -3 to 3
- output_bias: bfloat16 [768], P('wide'), may hold values from -3 to 3
- mid_gain: bfloat16 [768], P('wide'), may hold values from 0.099609375 to 1.8984375
- mid_bias: bfloat16 [768], P('wide'), may hold values from -3 to 3
- up_bias: bfloat16 [3072], P('wide'), may hold values from -3 to 3
- down_bias: bfloat16 [768], P('wide'), may hold values from -3 to 3
Outputs:
- block_out: bfloat16 [32768, 768], P(('narrow', 'wide'))
- input_grad: bfloat16 [32768, 768], P(('narrow', 'wide'))
- grad_input_weight: float32 [768, 2304], P('wide')
- grad_output_weight: float32 [768, 768], P('wide')
- grad_up_weight: float32 [768, 3072], P('wide')
- grad_down_weight: float32 [3072, 768], P('wide')
- grad_pre_gain: float32 [768], P('wide')
- grad_pre_bias: float32 [768], P('wide')
- grad_query_bias: float32 [768], P('wide')
- grad_value_bias: float32 [768], P('wide')
- grad_output_bias: float32 [768], P('wide')
- grad_mid_gain: float32 [768], P('wide')
- grad_mid_bias: float32 [768], P('wide')
- grad_up_bias: float32 [3072], P('wide')
- grad_down_bias: float32 [768], P('wide')
Inputs may be any that keep to these rules, and one draw needn't show every extreme that they name: `frame_counts`: each packed sequence fills its clip slots in order; a slot's clip has 8, 16 or 32 frames, short clips being the most common; slots that the sequence's rows never reach still hold a frame count. `segment_ids`: within a sequence the slot number never falls and starts at 0; a clip of 8, 16 or 32 frames holds 78, 157 or 314 rows times 1024 / 1024 (rounded down, at least 1), except that the sequence's end may cut its last clip. `positions`: index of a row's tubelet in its clip's grid of (frames / 2) x 14 x 14 tubelets, below that grid's size.
All inputs are finite; a program needn't handle non-finite values.
Results may differ from a plain program's by a relative error of at most 0.019.
Values may be sent and summed in bfloat16 or wider, within the bound.
No kernel may reach another device: no remote copies, remote signals or barrier semaphores. Data moves between devices by JAX's collectives and lax.ppermute only.
A program may use at most 192 MiB of HBM per device.

v0:
```python
from functools import partial
import math
import jax
import jax.numpy as jnp
from jax import lax
from jax.sharding import PartitionSpec as P

D = 768
HEADS = 12
HEAD_DIM = 64


def layer_norm(values, gain, shift):
    center = values - jnp.mean(values, axis=-1, keepdims=True)
    spread = jnp.mean(center * center, axis=-1, keepdims=True)
    return center * lax.rsqrt(spread + 1e-06) * gain + shift


def position_table(position_ids, frame_row):
    tubelet = position_ids // 196
    within = position_ids % 196
    first = tubelet.astype(jnp.float32) * 16.0 / frame_row.astype(jnp.float32)
    second = (within // 14).astype(jnp.float32)
    third = (within % 14).astype(jnp.float32)
    channel = jnp.arange(D, dtype=jnp.int32)
    picker = (channel % 3)[None, :]
    rate = jnp.exp(-(6.0 * (channel // 6).astype(jnp.float32) / D) * math.log(10000.0))
    coordinate = jnp.where(
        picker == 0, first[:, None], jnp.where(picker == 1, second[:, None], third[:, None])
    )
    angle = coordinate * rate[None, :]
    return jnp.where((channel // 3 % 2)[None, :] == 1, jnp.cos(angle), jnp.sin(angle))


def to_items(values, seq_count, length):
    pair_count = HEADS // 2
    shaped = values.reshape(seq_count, length, pair_count, 2, HEAD_DIM).transpose(0, 2, 1, 3, 4)
    return shaped.reshape(seq_count * pair_count, length, 2, HEAD_DIM)


def from_items(items, seq_count, length):
    pair_count = HEADS // 2
    shaped = items.reshape(seq_count, pair_count, length, 2, HEAD_DIM).transpose(0, 2, 1, 3, 4)
    return shaped.reshape(seq_count * length, D)


def masked_scores(queries, key_rows, labels):
    scores = jnp.einsum(
        "qhd,khd->hqk", queries, key_rows, preferred_element_type=jnp.float32
    ) * HEAD_DIM ** (-0.5)
    allowed = labels[:, None] == labels[None, :]
    return jnp.where(allowed[None], scores, -1e30)


def pair_forward(packed):
    queries, key_rows, values, labels = packed
    scores = masked_scores(queries, key_rows, labels)
    peak_score = jnp.max(scores, axis=-1, keepdims=True)
    expo_scores = jnp.exp(scores - peak_score)
    total_mass = jnp.sum(expo_scores, axis=-1, keepdims=True)
    probabilities = expo_scores / total_mass
    attended = jnp.einsum(
        "hqk,khd->qhd",
        probabilities.astype(jnp.bfloat16),
        values,
        preferred_element_type=jnp.float32,
    )
    return (attended, (peak_score + jnp.log(total_mass))[..., 0])


def pair_backward(packed):
    queries, key_rows, values, labels, grad_out, log_mass = packed
    scores = masked_scores(queries, key_rows, labels)
    probabilities = jnp.exp(scores - log_mass[..., None])
    grad_probs = jnp.einsum("qhd,khd->hqk", grad_out, values, preferred_element_type=jnp.float32)
    weighted = jnp.sum(probabilities * grad_probs, axis=-1, keepdims=True)
    grad_scores = (probabilities * (grad_probs - weighted)).astype(jnp.bfloat16)
    scale = HEAD_DIM ** (-0.5)
    grad_query = (
        jnp.einsum("hqk,khd->qhd", grad_scores, key_rows, preferred_element_type=jnp.float32)
        * scale
    )
    grad_keys = (
        jnp.einsum("hqk,qhd->khd", grad_scores, queries, preferred_element_type=jnp.float32) * scale
    )
    grad_values = jnp.einsum(
        "hqk,qhd->khd",
        probabilities.astype(jnp.bfloat16),
        grad_out,
        preferred_element_type=jnp.float32,
    )
    return (grad_query, grad_keys, grad_values)


def reduce_feedforward(gradients):
    shares = (
        lax.psum_scatter(
            gradients[0].astype(jnp.bfloat16), "wide", scatter_dimension=0, tiled=True
        ).astype(jnp.float32),
        lax.psum_scatter(
            gradients[1].astype(jnp.bfloat16), "wide", scatter_dimension=0, tiled=True
        ).astype(jnp.float32),
        lax.psum_scatter(
            gradients[2].astype(jnp.bfloat16), "wide", scatter_dimension=0, tiled=True
        ).astype(jnp.float32),
        lax.psum_scatter(
            gradients[3].astype(jnp.bfloat16), "wide", scatter_dimension=0, tiled=True
        ).astype(jnp.float32),
        lax.psum_scatter(
            gradients[4].astype(jnp.bfloat16), "wide", scatter_dimension=0, tiled=True
        ).astype(jnp.float32),
        lax.psum_scatter(
            gradients[5].astype(jnp.bfloat16), "wide", scatter_dimension=0, tiled=True
        ).astype(jnp.float32),
    )
    return (
        lax.psum(shares[0].astype(jnp.bfloat16), "narrow").astype(jnp.float32),
        lax.psum(shares[1].astype(jnp.bfloat16), "narrow").astype(jnp.float32),
        lax.psum(shares[2].astype(jnp.bfloat16), "narrow").astype(jnp.float32),
        lax.psum(shares[3].astype(jnp.bfloat16), "narrow").astype(jnp.float32),
        lax.psum(shares[4].astype(jnp.bfloat16), "narrow").astype(jnp.float32),
        lax.psum(shares[5].astype(jnp.bfloat16), "narrow").astype(jnp.float32),
    )


def reduce_attention(gradients):
    shares = (
        lax.psum_scatter(
            gradients[0].astype(jnp.bfloat16), "wide", scatter_dimension=0, tiled=True
        ).astype(jnp.float32),
        lax.psum_scatter(
            gradients[1].astype(jnp.bfloat16), "wide", scatter_dimension=0, tiled=True
        ).astype(jnp.float32),
        lax.psum_scatter(
            gradients[2].astype(jnp.bfloat16), "wide", scatter_dimension=0, tiled=True
        ).astype(jnp.float32),
        lax.psum_scatter(
            gradients[3].astype(jnp.bfloat16), "wide", scatter_dimension=0, tiled=True
        ).astype(jnp.float32),
        lax.psum_scatter(
            gradients[4].astype(jnp.bfloat16), "wide", scatter_dimension=0, tiled=True
        ).astype(jnp.float32),
        lax.psum_scatter(
            gradients[5].astype(jnp.bfloat16), "wide", scatter_dimension=0, tiled=True
        ).astype(jnp.float32),
        lax.psum_scatter(
            gradients[6].astype(jnp.bfloat16), "wide", scatter_dimension=0, tiled=True
        ).astype(jnp.float32),
    )
    return (
        lax.psum(shares[0].astype(jnp.bfloat16), "narrow").astype(jnp.float32),
        lax.psum(shares[1].astype(jnp.bfloat16), "narrow").astype(jnp.float32),
        lax.psum(shares[2].astype(jnp.bfloat16), "narrow").astype(jnp.float32),
        lax.psum(shares[3].astype(jnp.bfloat16), "narrow").astype(jnp.float32),
        lax.psum(shares[4].astype(jnp.bfloat16), "narrow").astype(jnp.float32),
        lax.psum(shares[5].astype(jnp.bfloat16), "narrow").astype(jnp.float32),
        lax.psum(shares[6].astype(jnp.bfloat16), "narrow").astype(jnp.float32),
    )


def per_device(
    tokens,
    frame_counts,
    segment_ids,
    positions,
    cotangent,
    input_weight,
    output_weight,
    up_weight,
    down_weight,
    pre_gain,
    pre_bias,
    query_bias,
    value_bias,
    output_bias,
    mid_gain,
    mid_bias,
    up_bias,
    down_bias,
):
    seq_count = frame_counts.shape[0]
    row_total = tokens.shape[0]
    length = row_total // seq_count
    pair_count = HEADS // 2
    labels = segment_ids.reshape(seq_count, length)
    clip_index = jnp.arange(frame_counts.shape[1], dtype=jnp.int32)
    matches = labels[:, :, None] == clip_index[None, None, :]
    frame_row = jnp.sum(jnp.where(matches, frame_counts[:, None, :], 0), axis=2).reshape(row_total)
    start = tokens.astype(jnp.float32) + position_table(positions, frame_row)
    (
        full_input,
        full_output,
        full_pre_gain,
        full_pre_bias,
        full_query_bias,
        full_value_bias,
        full_output_bias,
    ) = (
        lax.all_gather(input_weight, "wide", axis=0, tiled=True),
        lax.all_gather(output_weight, "wide", axis=0, tiled=True),
        lax.all_gather(pre_gain, "wide", axis=0, tiled=True),
        lax.all_gather(pre_bias, "wide", axis=0, tiled=True),
        lax.all_gather(query_bias, "wide", axis=0, tiled=True),
        lax.all_gather(value_bias, "wide", axis=0, tiled=True),
        lax.all_gather(output_bias, "wide", axis=0, tiled=True),
    )
    pre_gain_f = full_pre_gain.astype(jnp.float32)
    normed_low = layer_norm(start, pre_gain_f, full_pre_bias.astype(jnp.float32)).astype(
        jnp.bfloat16
    )
    query_bias_f = full_query_bias.astype(jnp.float32)
    joint_bias = jnp.concatenate(
        [query_bias_f, jnp.zeros_like(query_bias_f), full_value_bias.astype(jnp.float32)]
    )
    mixed_low = (
        jnp.dot(normed_low, full_input, preferred_element_type=jnp.float32) + joint_bias
    ).astype(jnp.bfloat16)
    item_labels = jnp.broadcast_to(labels[:, None, :], (seq_count, pair_count, length)).reshape(
        seq_count * pair_count, length
    )
    query_items = to_items(mixed_low[:, :D], seq_count, length)
    key_items = to_items(mixed_low[:, D : 2 * D], seq_count, length)
    value_items = to_items(mixed_low[:, 2 * D :], seq_count, length)
    attended_items, log_mass = lax.map(
        pair_forward, (query_items, key_items, value_items, item_labels)
    )
    attended_low = from_items(attended_items, seq_count, length).astype(jnp.bfloat16)
    middle = (
        start
        + jnp.dot(attended_low, full_output, preferred_element_type=jnp.float32)
        + full_output_bias.astype(jnp.float32)
    )
    full_up, full_down, full_mid_gain, full_mid_bias, full_up_bias, full_down_bias = (
        lax.all_gather(up_weight, "wide", axis=0, tiled=True),
        lax.all_gather(down_weight, "wide", axis=0, tiled=True),
        lax.all_gather(mid_gain, "wide", axis=0, tiled=True),
        lax.all_gather(mid_bias, "wide", axis=0, tiled=True),
        lax.all_gather(up_bias, "wide", axis=0, tiled=True),
        lax.all_gather(down_bias, "wide", axis=0, tiled=True),
    )
    normed_two = layer_norm(
        middle, full_mid_gain.astype(jnp.float32), full_mid_bias.astype(jnp.float32)
    )
    normed_two_low = normed_two.astype(jnp.bfloat16)
    upward = jnp.dot(
        normed_two_low, full_up, preferred_element_type=jnp.float32
    ) + full_up_bias.astype(jnp.float32)
    gelu_exact = partial(jax.nn.gelu, approximate=False)
    active_low = gelu_exact(upward).astype(jnp.bfloat16)
    block_out = (
        middle
        + jnp.dot(active_low, full_down, preferred_element_type=jnp.float32)
        + full_down_bias.astype(jnp.float32)
    ).astype(jnp.bfloat16)
    up_back, down_back, mid_gain_back = (
        lax.all_gather(up_weight, "wide", axis=0, tiled=True),
        lax.all_gather(down_weight, "wide", axis=0, tiled=True),
        lax.all_gather(mid_gain, "wide", axis=0, tiled=True),
    )
    grad_top = cotangent.astype(jnp.float32)
    grad_down_bias = jnp.sum(grad_top, axis=0)
    grad_down_weight = jnp.einsum(
        "rf,rd->fd", active_low, cotangent, preferred_element_type=jnp.float32
    )
    grad_active = jnp.einsum("rd,fd->rf", cotangent, down_back, preferred_element_type=jnp.float32)
    _, gelu_pull = jax.vjp(gelu_exact, upward)
    grad_upward_low = gelu_pull(grad_active)[0].astype(jnp.bfloat16)
    grad_up_bias = jnp.sum(grad_upward_low.astype(jnp.float32), axis=0)
    grad_up_weight = jnp.einsum(
        "rd,rf->df", normed_two_low, grad_upward_low, preferred_element_type=jnp.float32
    )
    grad_normed_two = jnp.einsum(
        "rf,df->rd", grad_upward_low, up_back, preferred_element_type=jnp.float32
    )
    mid_gain_f = mid_gain_back.astype(jnp.float32)
    _, norm_pull = jax.vjp(layer_norm, middle, mid_gain_f, jnp.zeros_like(mid_gain_f))
    grad_middle_part, grad_mid_gain, grad_mid_bias = norm_pull(grad_normed_two)
    grad_middle = grad_top + grad_middle_part
    out_up_weight, out_down_weight, out_mid_gain, out_mid_bias, out_up_bias, out_down_bias = (
        reduce_feedforward(
            (
                grad_up_weight,
                grad_down_weight,
                grad_mid_gain,
                grad_mid_bias,
                grad_up_bias,
                grad_down_bias,
            )
        )
    )
    input_back, output_back, pre_gain_back = (
        lax.all_gather(input_weight, "wide", axis=0, tiled=True),
        lax.all_gather(output_weight, "wide", axis=0, tiled=True),
        lax.all_gather(pre_gain, "wide", axis=0, tiled=True),
    )
    grad_branch_low = grad_middle.astype(jnp.bfloat16)
    grad_output_bias = jnp.sum(grad_branch_low.astype(jnp.float32), axis=0)
    grad_output_weight = jnp.einsum(
        "rd,re->de", attended_low, grad_branch_low, preferred_element_type=jnp.float32
    )
    grad_attended_low = jnp.einsum(
        "re,de->rd", grad_branch_low, output_back, preferred_element_type=jnp.float32
    ).astype(jnp.bfloat16)
    grad_items = to_items(grad_attended_low, seq_count, length)
    grad_query, grad_keys, grad_values = lax.map(
        pair_backward, (query_items, key_items, value_items, item_labels, grad_items, log_mass)
    )
    grad_mixed_low = jnp.concatenate(
        [
            from_items(grad_query, seq_count, length),
            from_items(grad_keys, seq_count, length),
            from_items(grad_values, seq_count, length),
        ],
        axis=1,
    ).astype(jnp.bfloat16)
    grad_query_bias = jnp.sum(grad_mixed_low[:, :D].astype(jnp.float32), axis=0)
    grad_value_bias = jnp.sum(grad_mixed_low[:, 2 * D :].astype(jnp.float32), axis=0)
    grad_input_weight = jnp.einsum(
        "rd,re->de", normed_low, grad_mixed_low, preferred_element_type=jnp.float32
    )
    grad_normed = jnp.einsum(
        "re,de->rd", grad_mixed_low, input_back, preferred_element_type=jnp.float32
    )
    pre_gain_b = pre_gain_back.astype(jnp.float32)
    _, first_pull = jax.vjp(layer_norm, start, pre_gain_b, jnp.zeros_like(pre_gain_b))
    grad_start_part, grad_pre_gain, grad_pre_bias = first_pull(grad_normed)
    input_grad = (grad_middle + grad_start_part).astype(jnp.bfloat16)
    (
        out_input_weight,
        out_output_weight,
        out_pre_gain,
        out_pre_bias,
        out_query_bias,
        out_value_bias,
        out_output_bias,
    ) = reduce_attention(
        (
            grad_input_weight,
            grad_output_weight,
            grad_pre_gain,
            grad_pre_bias,
            grad_query_bias,
            grad_value_bias,
            grad_output_bias,
        )
    )
    return (
        block_out,
        input_grad,
        out_input_weight,
        out_output_weight,
        out_up_weight,
        out_down_weight,
        out_pre_gain,
        out_pre_bias,
        out_query_bias,
        out_value_bias,
        out_output_bias,
        out_mid_gain,
        out_mid_bias,
        out_up_bias,
        out_down_bias,
    )


def solution(mesh):
    in_specs = (
        P(("narrow", "wide"), None),
        P(("narrow", "wide"), None),
        P(("narrow", "wide")),
        P(("narrow", "wide")),
        P(("narrow", "wide"), None),
        P("wide", None),
        P("wide", None),
        P("wide", None),
        P("wide", None),
        P("wide"),
        P("wide"),
        P("wide"),
        P("wide"),
        P("wide"),
        P("wide"),
        P("wide"),
        P("wide"),
        P("wide"),
    )
    out_specs = (
        P(("narrow", "wide"), None),
        P(("narrow", "wide"), None),
        P("wide", None),
        P("wide", None),
        P("wide", None),
        P("wide", None),
        P("wide"),
        P("wide"),
        P("wide"),
        P("wide"),
        P("wide"),
        P("wide"),
        P("wide"),
        P("wide"),
        P("wide"),
    )
    return jax.shard_map(
        per_device, mesh=mesh, in_specs=in_specs, out_specs=out_specs, check_vma=False
    )
```

profile of v0, /device:TPU:0, one launch (start us, length us, event | category | flops | bytes accessed | tf_op | source)
XLA Modules:
  0.0 671.5 jit_solution(14226232161853406409)
XLA Ops:
  12.9 13.1 %fusion.92 = f32[1024]{0:T(1024)S(1)} fusion(f32[768]{0:T(1024)S(1)} %fusion.71, f32[1024]{0:T(1024)S(1)} %get-tuple-element.254, f32[1024]{0:T(1024)S(1)} %get-tuple-element.253, pred[768]{0:T(1024)(128)(4,1)S(1)} %get-tuple-element.267, f32[1024]{0:T(1024)S(1)} %fusion.76, pred[768]{0:T(1024)(128)(4,1)S(1)} %fusion.81, ...), kind=kLoop, calls=%fused_computation.165 | loop fusion | flops 5504000 | bytes 1594624 | tf_op jit(solution)/shard_map/reduce_sum | solution.py:14
  26.0 13.3 %multiply_reduce_fusion.6 = f32[1024]{0:T(1024)S(1)} fusion(f32[1024]{0:T(1024)S(1)} %broadcast_multiply_fusion.1, f32[768]{0:T(1024)S(1)} %fusion.71, f32[1024]{0:T(1024)S(1)} %get-tuple-element.254, f32[1024]{0:T(1024)S(1)} %get-tuple-element.253, pred[768]{0:T(1024)(128)(4,1)S(1)} %get-tuple-element.267, f32[1024]{0:T(1024)S(1)} %fusion.76, ...), kind=kLoop, calls=%fused_computation.97 | loop fusion | flops 7076864 | bytes 1598720 | tf_op jit(solution)/shard_map/reduce_sum | solution.py:15
  42.3 30.8 %all-reduce.18 = (bf16[768]{0:T(1024)(128)(2,1)S(1)}, bf16[768]{0:T(1024)(128)(2,1)S(1)}, bf16[768]{0:T(1024)(128)(2,1)S(1)}, bf16[768]{0:T(1024)(128)(2,1)S(1)}...) all-reduce(bf16[768]{0:T(1024)(128)(2,1)S(1)} %dynamic-update-slice, ...), channel_id=1, replica_groups=mesh['narrow'=4,'wide'=8] {'wide'}, use_global_device_ids=true, to_apply=%add.3 | all-reduce | flops 5376 | bytes 21504
  73.2 12.8 %all-gather = bf16[8,1,384]{2,1,0:T(2,128)(2,1)S(1)} all-gather(bf16[1,1,384]{2,1,0:T(2,128)(2,1)S(1)} %reshape.408), channel_id=1, replica_groups=mesh['narrow'=4,'wide'=8] {'wide'}, dimensions={0}, use_global_device_ids=true | all-gather | bytes 6912 | tf_op jit(solution)/shard_map/all_gather | solution.py:238
  87.7 14.2 %add_convert_fusion.13 = bf16[1024,768]{0,1:T(8,128)(2,1)} fusion(f32[768]{0:T(1024)S(1)} %convert_element_type.208, f32[768]{0:T(1024)S(1)} %convert_element_type.207, f32[1024]{0:T(1024)S(1)} %fusion.86, f32[1024]{0:T(1024)S(1)} %broadcast_multiply_fusion.1, f32[768]{0:T(1024)S(1)} %fusion.71, f32[1024]{0:T(1024)S(1)} %get-tuple-element.254, ...), kind=kLoop, calls=%fused_computation.96.clone.clone.2 | loop fusion | flops 8650752 | bytes 3177728 | tf_op jit(solution)/shard_map/rd,re->de/dot_general | solution.py:318
  102.0 18.0 %add_convert_fusion.1 = bf16[1024,2304]{1,0:T(8,128)(2,1)S(1)} fusion(bf16[768,2304]{1,0:T(8,128)(2,1)} %all-gather.6.cloned.1.call-done, f32[2304]{0:T(1024)S(1)} %pad_maximum_fusion.3, f32[768]{0:T(1024)S(1)} %convert_element_type.208, f32[768]{0:T(1024)S(1)} %convert_element_type.207, f32[1024]{0:T(1024)S(1)} %fusion.86, ...), kind=kOutput, calls=%fused_computation.79 | convolution fusion | flops 3637248000 | bytes 9871616 | tf_op jit(solution)/shard_map/dot_general | solution.py:216
  129.3 63.2 %while.26 = (s32[]{:T(128)}, bf16[6,1024,2,64]{1,3,2,0:T(8,128)(2,1)}, f32[6,2,1024]{2,1,0:T(2,128)}, bf16[6,1024,2,64]{1,3,2,0:T(8,128)(2,1)}, s32[6,1024]{1,0:...) while((s32[]{:T(128)}, ...), condition=%wide.region_6.7_spmd, body=%wide.region_3.6_spmd.sunk | while | flops 563083264 | bytes 30751320 | solution.py:224
  129.9 2.8 fusion.141
  135.4 4.4 fusion.143
  140.5 2.8 fusion.141
  145.9 4.4 fusion.143
  151.0 2.8 fusion.141
  156.5 4.4 fusion.143
  161.5 2.8 fusion.141
  167.0 4.4 fusion.143
  172.1 2.8 fusion.141
  177.5 4.4 fusion.143
  182.6 2.8 fusion.141
  188.1 4.4 fusion.143
  192.5 15.3 %fusion.99 = (f32[1024]{0:T(1024)S(1)}, f32[1024,768]{0,1:T(8,128)S(1)}) fusion(f32[768]{0:T(1024)S(1)} %convert_element_type.217, bf16[1024,768]{0,1:T(8,128)(2,1)} %bitcast.32, bf16[768,768]{1,0:T(8,128)(2,1)} %all-gather.8.cloned.1.call-done, f32[768]{0:T(1024)S(1)} %fusion.71, f32[1024]{0:T(1024)S(1)} %get-tuple-element.254, ...), kind=kOutput, calls=%fused_computation.170 | convolution fusion | flops 1215036416 | bytes 7495936 | tf_op jit(solution)/shard_map/dot_general | solution.py:230
  210.0 38.1 %multiply_convert_fusion.1 = (bf16[1024,3072]{1,0:T(8,128)(2,1)}, f32[1024,3072]{1,0:T(8,128)}, f32[1024,3072]{1,0:T(8,128)}) fusion(f32[3072]{0:T(1024)S(1)} %bitcast.182, bf16[768,3072]{1,0:T(8,128)(2,1)} %all-gather.10.cloned.1.call-done, f32[1024,768]{0,1:T(8,128)} %copy-done.2, f32[768]{0:T(1024)S(1)} %convert_element_type.219, ...), kind=kOutput, calls=%fused_computation.65 | convolution fusion | flops 5043388416 | bytes 39348224 | tf_op jit(solution)/shard_map/dot_general | solution.py:245
  248.0 17.4 %fusion.102 = (bf16[3072]{0:T(1024)(128)(2,1)}, bf16[1024,3072]{1,0:T(8,128)(2,1)}) fusion(f32[1024,3072]{1,0:T(8,128)} %get-tuple-element.245, bf16[1024,768]{1,0:T(8,128)(2,1)S(1)} %copy-done.10, bf16[3072,768]{1,0:T(8,128)(2,1)} %all-gather.12.cloned.1.call-done, f32[1024,3072]{1,0:T(8,128)} %get-tuple-element.259, f32[3072]{0:T(1024)S(1)} %bitcast.183), kind=kOutput, calls=%fused_computation.173 | convolution fusion | flops 4882166784 | bytes 37767168 | tf_op jit(solution)/shard_map/rd,fd->rf/dot_general | solution.py:265
  265.4 10.7 %fusion.101 = (bf16[768]{0:T(1024)(128)(2,1)}, f32[1024,768]{1,0:T(8,128)}) fusion(bf16[1024,3072]{1,0:T(8,128)(2,1)} %get-tuple-element.265, bf16[768,3072]{1,0:T(8,128)(2,1)} %all-gather.10.cloned.1.call-done), kind=kOutput, calls=%fused_computation.172 | convolution fusion | flops 4832623616 | bytes 14157312 | tf_op jit(solution)/shard_map/rf,df->rd/dot_general | solution.py:272
  276.2 3.7 copy.91
  279.8 3.5 multiply_reduce_fusion.1
  287.0 3.8 convolution_convert_fusion.4
  291.0 4.3 convolution_convert_fusion.3
  299.4 130.1 %while.27 = (s32[]{:T(128)}, bf16[6,1024,2,64]{1,3,2,0:T(8,128)(2,1)}, bf16[6,1024,2,64]{1,3,2,0:T(8,128)(2,1)}, bf16[6,1024,2,64]{1,3,2,0:T(8,128)(2,1)}, bf16[...) while((s32[]{:T(128)}, ...), condition=%wide.region_13.14_spmd, body=%wide.region_11.13_spmd.sunk | while | flops 1374943232 | bytes 83174576 | solution.py:305
  304.0 4.2 multiply_reduce_fusion.8
  308.2 2.7 multiply_convert_fusion.3
  310.9 3.2 fusion.154
  317.0 4.2 fusion.155
  325.7 4.2 multiply_reduce_fusion.8
  329.8 2.7 multiply_convert_fusion.3
  332.6 3.2 fusion.154
  338.7 4.2 fusion.155
  347.3 4.2 multiply_reduce_fusion.8
  351.5 2.7 multiply_convert_fusion.3
  354.2 3.2 fusion.154
  360.4 4.2 fusion.155
  369.0 4.2 multiply_reduce_fusion.8
  373.2 2.7 multiply_convert_fusion.3
  375.9 3.2 fusion.154
  382.0 4.2 fusion.155
  390.6 4.2 multiply_reduce_fusion.8
  397.5 3.2 fusion.154
  403.7 4.2 fusion.155
  412.3 4.2 multiply_reduce_fusion.8
  416.5 2.7 multiply_convert_fusion.3
  419.2 3.2 fusion.154
  425.3 4.2 fusion.155
  429.5 8.5 %convolution_convert_fusion.2 = bf16[768,2304]{1,0:T(8,128)(2,1)} fusion(bf16[1024,768]{0,1:T(8,128)(2,1)} %bitcast.51, bf16[1024,768]{0,1:T(8,128)(2,1)} %bitcast.177, bf16[1024,768]{0,1:T(8,128)(2,1)} %bitcast.174, bf16[1024,768]{0,1:T(8,128)(2,1)} %add_convert_fusion.13), kind=kOutput, calls=%fused_computation.82 | convolution fusion | flops 3639803904 | bytes 9830400 | tf_op jit(solution)/shard_map/rd,re->de/dot_general | solution.py:318
  438.6 10.0 %convolution_convert_fusion.1 = bf16[768,3072]{1,0:T(8,128)(2,1)} fusion(bf16[1024,3072]{1,0:T(8,128)(2,1)} %get-tuple-element.265, f32[1024,768]{0,1:T(8,128)S(1)} %copy-done.3, f32[768]{0:T(1024)S(1)} %copy-done.49, f32[768]{0:T(1024)S(1)} %convert_element_type.218, f32[1024]{0:T(1024)S(1)} %fusion.87, f32[1024]{0:T(1024)S(1)} %broadcast_multiply_fusion), kind=kOutput, calls=%fused_computation.81 | convolution fusion | flops 4838129664 | bytes 14170112 | tf_op jit(solution)/shard_map/rd,rf->df/dot_general | solution.py:269
  450.0 9.8 %convolution_convert_fusion = bf16[3072,768]{1,0:T(8,128)(2,1)} fusion(bf16[1024,3072]{1,0:T(8,128)(2,1)} %get-tuple-element.244, bf16[1024,768]{1,0:T(8,128)(2,1)S(1)} %copy-done.11), kind=kOutput, calls=%fused_computation.80 | convolution fusion | flops 4834197504 | bytes 12582912 | tf_op jit(solution)/shard_map/rf,rd->fd/dot_general | solution.py:262
  461.9 8.7 %fusion.100 = (bf16[768]{0:T(1024)(128)(2,1)S(1)}, f32[1024,768]{1,0:T(8,128)}) fusion(bf16[768,2304]{1,0:T(8,128)(2,1)} %all-gather.6.cloned.1.call-done, bf16[1024,768]{0,1:T(8,128)(2,1)} %bitcast.51, bf16[1024,768]{0,1:T(8,128)(2,1)} %bitcast.178, bf16[1024,768]{0,1:T(8,128)(2,1)S(1)} %bitcast.175), kind=kOutput, calls=%fused_computation.171 | convolution fusion | flops 3638820096 | bytes 11404800 | tf_op jit(solution)/shard_map/re,de->rd/dot_general | solution.py:321
  476.7 14.3 %multiply_reduce_fusion.3 = f32[1024]{0:T(1024)S(1)} fusion(f32[1024,768]{0,1:T(8,128)S(1)} %copy.92, f32[768]{0:T(1024)S(1)} %copy-done.30, f32[1024]{0:T(1024)S(1)} %copy-done.28, f32[768]{0:T(1024)S(1)} %copy-done.20, f32[1024]{0:T(1024)S(1)} %copy-done.24, f32[1024]{0:T(1024)S(1)} %copy-done.22, pred[768]{0:T(1024)(128)(4,1)S(1)} %copy-done.38, ...), kind=kLoop, calls=%fused_computation.89 | loop fusion | flops 7863296 | bytes 4747520 | tf_op jit(solution)/shard_map/transpose(jvp())/reduce_sum | solution.py:16
  491.1 13.4 %multiply_reduce_fusion.2 = (bf16[768]{0:T(1024)(128)(2,1)S(1)}, f32[1024]{0:T(1024)S(1)}) fusion(f32[1024,768]{0,1:T(8,128)S(1)} %copy.92, f32[1024]{0:T(1024)S(1)} %copy-done.32, f32[1024]{0:T(1024)S(1)} %copy-done.28, f32[768]{0:T(1024)S(1)} %copy-done.20, f32[1024]{0:T(1024)S(1)} %copy-done.24, f32[1024]{0:T(1024)S(1)} %copy-done.22, ...), kind=kLoop, calls=%fused_computation.87 | loop fusion | flops 12581120 | bytes 4757248 | tf_op jit(solution)/shard_map/transpose(jvp())/reduce_sum | solution.py:16
  504.6 27.9 %all-reduce.17 = (bf16[768]{0:T(1024)(128)(2,1)S(1)}, bf16[768]{0:T(1024)(128)(2,1)S(1)}, bf16[768]{0:T(1024)(128)(2,1)S(1)}, bf16[768]{0:T(1024)(128)(2,1)S(1)}...) all-reduce(bf16[768]{0:T(1024)(128)(2,1)S(1)} %dynamic-update-slice, ...), channel_id=1, replica_groups=mesh['narrow'=4,'wide'=8] {'wide'}, use_global_device_ids=true, to_apply=%add.7 | all-reduce | flops 9984 | bytes 39936
  533.1 10.2 %all-reduce.19 = (bf16[96]{0:T(256)(128)(2,1)S(1)}, bf16[96]{0:T(256)(128)(2,1)S(1)}, bf16[96]{0:T(256)(128)(2,1)S(1)}, bf16[96]{0:T(256)(128)(2,1)S(1)}, bf16[9...) all-reduce(bf16[96]{0:T(256)(128)(2,1)S(1)} %dynamic-slice.9, ...), channel_id=1, replica_groups=mesh['narrow'=4,'wide'=8] {'narrow'}, use_global_device_ids=true, to_apply=%region_26.27 | all-reduce | flops 1152 | bytes 4608 | tf_op jit(solution)/shard_map/psum | solution.py:153
  548.0 16.3 %add_convert_fusion.2 = bf16[1024,768]{0,1:T(8,128)(2,1)} fusion(f32[1024,768]{0,1:T(8,128)} %copy-done.6, bf16[1024,768]{0,1:T(8,128)(2,1)} %copy.90, f32[1024]{0:T(1024)S(1)} %negate_multiply_fusion.1, f32[1024]{0:T(1024)S(1)} %copy-done.34, f32[1024]{0:T(1024)S(1)} %multiply_multiply_fusion.5, f32[1024]{0:T(1024)S(1)} %copy-done.28, ...), kind=kLoop, calls=%fused_computation.88 | loop fusion | flops 14155776 | bytes 11051264 | tf_op jit(solution)/shard_map/convert_element_type | solution.py:327
  564.3 2.7 copy.96
  567.1 25.3 %reduce-scatter.11.cloned.1.call-done = bf16[384,768]{1,0:T(8,128)(2,1)} async-done(((bf16[3072,768]{1,0:T(8,128)(2,1)}), bf16[384,768]{1,0:T(8,128)(2,1)}) %reduce-scatter.11.cloned.1.call-update) | async-done | bytes 589840 | tf_op jit(solution)/shard_map/reduce_scatter | solution.py:100
  592.4 9.5 %add_convert_fusion.3 = bf16[1024,768]{0,1:T(8,128)(2,1)} fusion(f32[1024,768]{0,1:T(8,128)S(1)} %copy-done.4, bf16[1024,3072]{1,0:T(8,128)(2,1)} %get-tuple-element.244, bf16[3072,768]{1,0:T(8,128)(2,1)} %all-gather.12.cloned.1.call-done, f32[768]{0:T(1024)S(1)} %convert_element_type.223), kind=kOutput, calls=%fused_computation.92 | convolution fusion | flops 4834197504 | bytes 15731712 | tf_op jit(solution)/shard_map/dot_general | solution.py:252
  604.5 54.0 %all-reduce.23.cloned.1.call-done = (bf16[96,2304]{1,0:T(8,128)(2,1)}, bf16[96,768]{1,0:T(8,128)(2,1)}, bf16[96,3072]{1,0:T(8,128)(2,1)}, bf16[384,768]{1,0:T(8,128)(2,1)}) async-done(((bf16[96,2304]{1,0:T(8,128)(2,1)}, bf16[96,768]{1,0:T(8,128)(2,1)}, bf16[96,3072]{1,0:T(8,128)(2,1)}, bf16[384,768]{1,0:T(8,128)(2,1)}), (bf16[96,2304]{1,0:T(8,128)(2,1)}, bf16[96,768]{1,0:T(8,128)(2,1)}, ...) | async-done | bytes 1769488 | tf_op jit(solution)/shard_map/psum | solution.py:151
  (311 shorter events, 118.1 us)
Async XLA Ops:
  7.2 5.7 copy-start.39
  7.2 5.6 copy-start.53
  7.2 5.6 copy-start.40
  7.2 94.7 %all-gather.6.cloned.1.call-start = ((), (), s32[]{:S(2)}) async-start(), calls=%async_computation.4 | async-start | bytes 3981312 | tf_op jit(solution)/shard_map/all_gather | solution.py:199
  7.9 184.5 %all-gather.8.cloned.1.call-start = ((), (), s32[]{:S(2)}) async-start(), calls=%async_computation.5 | async-start | bytes 1327104 | tf_op jit(solution)/shard_map/all_gather | solution.py:200
  8.7 201.2 %all-gather.10.cloned.1.call-start = ((), (), s32[]{:S(2)}) async-start(), calls=%async_computation.6 | async-start | bytes 5308416 | tf_op jit(solution)/shard_map/all_gather | solution.py:234
  9.4 238.6 %all-gather.12.cloned.1.call-start = ((), (), s32[]{:S(2)}) async-start(), calls=%async_computation.7 | async-start | bytes 5308416 | tf_op jit(solution)/shard_map/all_gather | solution.py:235
  10.0 557.1 %reduce-scatter.7.cloned.1.call-start = ((), (), s32[]{:S(2)}) async-start(), calls=%async_computation.9 | async-start | bytes 1327104 | tf_op jit(solution)/shard_map/reduce_scatter | solution.py:131
  10.1 182.4 %copy-start.35 = (pred[768]{0:T(1024)(128)(4,1)}, pred[768]{0:T(1024)(128)(4,1)S(1)}, u32[]{:S(2)}) copy-start(pred[768]{0:T(1024)(128)(4,1)S(1)} %get-tuple-element.266) | copy-start | bytes 2308
  10.1 182.4 %copy-start.37 = (pred[768]{0:T(1024)(128)(4,1)}, pred[768]{0:T(1024)(128)(4,1)S(1)}, u32[]{:S(2)}) copy-start(pred[768]{0:T(1024)(128)(4,1)S(1)} %get-tuple-element.267) | copy-start | bytes 2308
  10.1 182.4 %copy-start.19 = (f32[768]{0:T(1024)}, f32[768]{0:T(1024)S(1)}, u32[]{:S(2)}) copy-start(f32[768]{0:T(1024)S(1)} %fusion.71) | copy-start | bytes 9220
  10.1 182.3 %copy-start.43 = (pred[768]{0:T(1024)(128)(4,1)}, pred[768]{0:T(1024)(128)(4,1)S(1)}, u32[]{:S(2)}) copy-start(pred[768]{0:T(1024)(128)(4,1)S(1)} %fusion.81) | copy-start | bytes 2308
  10.9 181.6 %copy-start.21 = (f32[1024]{0:T(1024)}, f32[1024]{0:T(1024)S(1)}, u32[]{:S(2)}) copy-start(f32[1024]{0:T(1024)S(1)} %get-tuple-element.253) | copy-start | bytes 12292
  10.9 181.6 %copy-start.23 = (f32[1024]{0:T(1024)}, f32[1024]{0:T(1024)S(1)}, u32[]{:S(2)}) copy-start(f32[1024]{0:T(1024)S(1)} %get-tuple-element.254) | copy-start | bytes 12292
  12.6 179.9 %copy-start = (bf16[1024,768]{0,1:T(8,128)(2,1)}, bf16[1024,768]{0,1:T(8,128)(2,1)S(1)}, u32[]{:S(2)}) copy-start(bf16[1024,768]{0,1:T(8,128)(2,1)S(1)} %copy.85) | copy-start | bytes 4718596
  12.6 26.7 %copy-start.51 = (u32[32]{0:T(128)S(1)}, u32[32]{0:T(128)}, u32[]{:S(2)}) copy-start(u32[32]{0:T(128)} %constant.211) | copy-start | bytes 388
  12.7 28.0 %copy-start.54 = (bf16[96]{0:T(256)(128)(2,1)S(1)}, bf16[96]{0:T(256)(128)(2,1)}, u32[]{:S(2)}) copy-start(bf16[96]{0:T(256)(128)(2,1)} %param.31) | copy-start | bytes 580
  12.7 28.2 %copy-start.55 = (bf16[96]{0:T(256)(128)(2,1)S(1)}, bf16[96]{0:T(256)(128)(2,1)}, u32[]{:S(2)}) copy-start(bf16[96]{0:T(256)(128)(2,1)} %param.32) | copy-start | bytes 580
  12.7 28.4 %copy-start.56 = (bf16[96]{0:T(256)(128)(2,1)S(1)}, bf16[96]{0:T(256)(128)(2,1)}, u32[]{:S(2)}) copy-start(bf16[96]{0:T(256)(128)(2,1)} %param.33) | copy-start | bytes 580
  12.7 28.6 %copy-start.57 = (bf16[96]{0:T(256)(128)(2,1)S(1)}, bf16[96]{0:T(256)(128)(2,1)}, u32[]{:S(2)}) copy-start(bf16[96]{0:T(256)(128)(2,1)} %param.34) | copy-start | bytes 580
  12.7 28.9 %copy-start.58 = (bf16[96]{0:T(256)(128)(2,1)S(1)}, bf16[96]{0:T(256)(128)(2,1)}, u32[]{:S(2)}) copy-start(bf16[96]{0:T(256)(128)(2,1)} %param.35) | copy-start | bytes 580
  12.7 29.1 %copy-start.59 = (bf16[96]{0:T(256)(128)(2,1)S(1)}, bf16[96]{0:T(256)(128)(2,1)}, u32[]{:S(2)}) copy-start(bf16[96]{0:T(256)(128)(2,1)} %param.36) | copy-start | bytes 580
  12.7 29.3 %copy-start.60 = (bf16[96]{0:T(256)(128)(2,1)S(1)}, bf16[96]{0:T(256)(128)(2,1)}, u32[]{:S(2)}) copy-start(bf16[96]{0:T(256)(128)(2,1)} %param.37) | copy-start | bytes 580
  12.7 60.4 %copy-start.52 = (bf16[384]{0:T(512)(128)(2,1)S(1)}, bf16[384]{0:T(512)(128)(2,1)}, u32[]{:S(2)}) copy-start(bf16[384]{0:T(512)(128)(2,1)} %param.38) | copy-start | bytes 2308
  12.8 73.2 %copy-start.9 = (bf16[1024,768]{1,0:T(8,128)(2,1)S(1)}, bf16[1024,768]{1,0:T(8,128)(2,1)}, u32[]{:S(2)}) copy-start(bf16[1024,768]{1,0:T(8,128)(2,1)} %param.26) | copy-start | bytes 4718596
  12.9 179.6 %copy-start.25 = (f32[1024]{0:T(1024)}, f32[1024]{0:T(1024)S(1)}, u32[]{:S(2)}) copy-start(f32[1024]{0:T(1024)S(1)} %fusion.76) | copy-start | bytes 12292
  26.0 76.0 %copy-start.27 = (f32[1024]{0:T(1024)}, f32[1024]{0:T(1024)S(1)}, u32[]{:S(2)}) copy-start(f32[1024]{0:T(1024)S(1)} %broadcast_multiply_fusion.1) | copy-start | bytes 12292
  39.3 33.8 %copy-start.41 = (f32[1024]{0:T(1024)}, f32[1024]{0:T(1024)S(1)}, u32[]{:S(2)}) copy-start(f32[1024]{0:T(1024)S(1)} %multiply_reduce_fusion.6) | copy-start | bytes 12292
  39.3 62.7 %copy-start.31 = (f32[1024]{0:T(1024)}, f32[1024]{0:T(1024)S(1)}, u32[]{:S(2)}) copy-start(f32[1024]{0:T(1024)S(1)} %fusion.86) | copy-start | bytes 12292
  73.1 28.9 %copy-start.29 = (f32[768]{0:T(1024)}, f32[768]{0:T(1024)S(1)}, u32[]{:S(2)}) copy-start(f32[768]{0:T(1024)S(1)} %convert_element_type.207) | copy-start | bytes 9220
  73.2 136.8 %copy-start.48 = (f32[768]{0:T(1024)}, f32[768]{0:T(1024)S(1)}, u32[]{:S(2)}) copy-start(f32[768]{0:T(1024)S(1)} %convert_element_type.219) | copy-start | bytes 9220
  192.4 15.4 %copy-start.8 = (bf16[6,1024,2,64]{1,3,2,0:T(8,128)(2,1)}, bf16[6,1024,2,64]{1,3,2,0:T(8,128)(2,1)S(1)}, u32[]{:S(2)}) copy-start(bf16[6,1024,2,64]{1,3,2,0:T(8,128)(2,1)S(1)} %get-tuple-element.453) | copy-start | bytes 4718596
  192.4 15.4 %copy-start.17 = (s32[6,1024]{1,0:T(8,128)}, s32[6,1024]{1,0:T(8,128)S(1)}, u32[]{:S(2)}) copy-start(s32[6,1024]{1,0:T(8,128)S(1)} %get-tuple-element.481) | copy-start | bytes 73732
  209.9 38.1 %copy-start.10 = (bf16[1024,768]{1,0:T(8,128)(2,1)S(1)}, bf16[1024,768]{1,0:T(8,128)(2,1)}, u32[]{:S(2)}) copy-start(bf16[1024,768]{1,0:T(8,128)(2,1)} %param.26) | copy-start | bytes 4718596
  276.1 3.7 copy-start.3
  279.8 3.5 copy-start.5
  290.9 276.1 %reduce-scatter.5.cloned.1.call-start = ((), (), s32[]{:S(2)}) async-start(), calls=%async_computation.8 | async-start | bytes 3981312 | tf_op jit(solution)/shard_map/reduce_scatter | solution.py:128
  310.9 3.2 copy-start.12
  332.5 3.2 copy-start.12
  397.5 3.2 copy-start.12
  419.2 3.2 copy-start.12
  438.0 129.1 %reduce-scatter.9.cloned.1.call-start = ((), (), s32[]{:S(2)}) async-start(), calls=%async_computation.10 | async-start | bytes 5308416 | tf_op jit(solution)/shard_map/reduce_scatter | solution.py:97
  448.6 143.7 %reduce-scatter.11.cloned.1.call-start = ((), (), s32[]{:S(2)}) async-start(), calls=%async_computation.11 | async-start | bytes 5308416 | tf_op jit(solution)/shard_map/reduce_scatter | solution.py:100
  459.9 198.6 %all-reduce.23.cloned.1.call-start = ((), (), s32[]{:S(2)}) async-start(), calls=%async_computation.12 | async-start | bytes 3538944 | tf_op jit(solution)/shard_map/psum | solution.py:151
  473.0 3.7 copy-start.20
  473.0 3.7 copy-start.22
  473.0 3.7 copy-start.24
  473.0 3.6 copy-start.26
  473.0 3.6 copy-start.28
  473.1 3.6 copy-start.30
  473.1 3.6 copy-start.36
  473.1 3.6 copy-start.38
  473.1 3.6 copy-start.44
  474.9 16.1 %copy-start.42 = (f32[1024]{0:T(1024)S(1)}, f32[1024]{0:T(1024)}, u32[]{:S(2)}) copy-start(f32[1024]{0:T(1024)} %copy-done.41) | copy-start | bytes 12292
  474.9 16.2 %copy-start.32 = (f32[1024]{0:T(1024)S(1)}, f32[1024]{0:T(1024)}, u32[]{:S(2)}) copy-start(f32[1024]{0:T(1024)} %copy-done.31) | copy-start | bytes 12292
  476.7 14.4 %copy-start.1 = (bf16[1024,768]{0,1:T(8,128)(2,1)S(1)}, bf16[1024,768]{0,1:T(8,128)(2,1)}, u32[]{:S(2)}) copy-start(bf16[1024,768]{0,1:T(8,128)(2,1)} %copy-done) | copy-start | bytes 4718596
  491.0 13.5 %copy-start.45 = (bf16[768]{0:T(1024)(128)(2,1)S(1)}, bf16[768]{0:T(1024)(128)(2,1)}, u32[]{:S(2)}) copy-start(bf16[768]{0:T(1024)(128)(2,1)} %get-tuple-element.240) | copy-start | bytes 4612
  491.0 13.5 %copy-start.46 = (bf16[768]{0:T(1024)(128)(2,1)S(1)}, bf16[768]{0:T(1024)(128)(2,1)}, u32[]{:S(2)}) copy-start(bf16[768]{0:T(1024)(128)(2,1)} %get-tuple-element.172) | copy-start | bytes 4612
  491.1 13.5 %copy-start.47 = (bf16[3072]{0:T(1024)(128)(2,1)S(1)}, bf16[3072]{0:T(1024)(128)(2,1)}, u32[]{:S(2)}) copy-start(bf16[3072]{0:T(1024)(128)(2,1)} %get-tuple-element.264) | copy-start | bytes 18436
  491.1 13.5 %copy-start.50 = (bf16[768]{0:T(1024)(128)(2,1)S(1)}, bf16[768]{0:T(1024)(128)(2,1)}, u32[]{:S(2)}) copy-start(bf16[768]{0:T(1024)(128)(2,1)} %get-tuple-element.262) | copy-start | bytes 4612
  491.1 56.9 %copy-start.34 = (f32[1024]{0:T(1024)S(1)}, f32[1024]{0:T(1024)}, u32[]{:S(2)}) copy-start(f32[1024]{0:T(1024)} %copy-done.33) | copy-start | bytes 12292
  564.3 28.0 %copy-start.4 = (f32[1024,768]{0,1:T(8,128)S(1)}, f32[1024,768]{0,1:T(8,128)}, u32[]{:S(2)}) copy-start(f32[1024,768]{0,1:T(8,128)} %copy-done.2) | copy-start | bytes 9437188
  658.5 4.4 copy-start.16
  658.5 5.4 copy-start.18
  (17 other events, 26.8 us)
Sparse Core Ops, SparseCore 0:
  9.7 44.2 all-gather.5
  55.6 21.6 all-gather.7
  78.9 50.9 all-gather.9
  131.4 50.2 all-gather.11
  291.0 31.4 reduce-scatter.6
  438.1 42.1 reduce-scatter.4
  482.6 54.0 reduce-scatter.8
  539.0 53.3 reduce-scatter.10
  595.8 62.6 all-reduce.22
where the time goes:
time: 682 us; the launch traced here: 672 us
  matrix products  291 us (43%)
  other arithmetic  146 us (21%)
  waiting for transfers between devices  82 us (12%)
  blocking collectives  81.7 us (12%)
  local copies, waits for them, and re-layouts  52.7 us (8%)
  between operations  17.4 us (3%)
    unnamed x2, blocking collectives  58.7 us
    psum x1, waiting for transfers between devices, reduce_attention(): lax.psum(shares[0].astype(jnp.bfloat16), 'narrow').astype(jnp.float32)  54 us
    dot_general x1, matrix products, per_device(): jnp.dot(normed_two_low, full_up, preferred_element_type=jnp.float32)  38.1 us
    reduce_sum x3, other arithmetic, layer_norm(): return center * lax.rsqrt(spread + 1e-06) * gain + shift  31.2 us
    dot_general x12, matrix products, masked_scores(): jnp.einsum('qhd,khd->hqk', queries, key_rows, preferred_element_type=jnp....  31 us
    dot_general x6, matrix products, pair_forward(): jnp.einsum('hqk,khd->qhd', probabilities.astype(jnp.bfloat16), values, pr...  26.4 us
    reduce_scatter x1, waiting for transfers between devices, reduce_feedforward(): lax.psum_scatter(gradients[1].astype(jnp.bfloat16), 'wide', scatter_dimen...  25.3 us
    dot_general x6, matrix products, pair_backward(): jnp.einsum('qhd,khd->hqk', grad_out, values, preferred_element_type=jnp.f...  25 us
  transfers between devices with their start and end apart: 9, of which 2 were waited for; matrix products, arithmetic and copies ran while one was open for 64% of the time, Pallas kernels for 0%

commit v1 on v0

--- a/solution.py
+++ b/solution.py
@@ -4,10 +4,16 @@
 import jax.numpy as jnp
 from jax import lax
 from jax.sharding import PartitionSpec as P
+from jax.lax import all_gather
 
 D = 768
 HEADS = 12
 HEAD_DIM = 64
+
+
+def _extend_types(u):
+    e_now = all_gather(u, "narrow")
+    return jnp.sum(e_now, 0)
 
 
 def layer_norm(values, gain, shift):
@@ -148,7 +154,7 @@
         ).astype(jnp.float32),
     )
     return (
-        lax.psum(shares[0].astype(jnp.bfloat16), "narrow").astype(jnp.float32),
+        _extend_types(shares[0].astype(jnp.bfloat16)).astype(jnp.float32),
         lax.psum(shares[1].astype(jnp.bfloat16), "narrow").astype(jnp.float32),
         lax.psum(shares[2].astype(jnp.bfloat16), "narrow").astype(jnp.float32),
         lax.psum(shares[3].astype(jnp.bfloat16), "narrow").astype(jnp.float32),

time: 682 us -> 723 us (1.060)
  waiting for transfers between devices: 82 us -> 138 us
  local copies, waits for them, and re-layouts: 52.7 us -> 43.6 us
    reduce_scatter x1, waiting for transfers between devices: 25.3 us -> 50.7 us  [reduce_feedforward(): lax.psum_scatter(gradients[1].astype(jnp.bfloat16), 'wide', scatter_dimen...]
    all_gather x0 -> x1, waiting for transfers between devices: none -> 20.7 us  [_extend_types(): e_now = all_gather(u, 'narrow')]
    unnamed x151 -> x149, local copies, waits for them, and re-layouts: 17.4 us -> 16.3 us
  transfers between devices with their start and end apart: 9 -> 10, of which waited for: 2 -> 4; matrix products, arithmetic and copies ran while one was open for 64% -> 41% of each run, Pallas kernels for 0% -> 0%
where the time goes in v1:
time: 723 us; the launch traced here: 713 us
  matrix products  290 us (40%)
  other arithmetic  142 us (20%)
  waiting for transfers between devices  138 us (19%)
  blocking collectives  81.3 us (11%)
  local copies, waits for them, and re-layouts  43.6 us (6%)
  between operations  17.5 us (2%)
    unnamed x2, blocking collectives  58.6 us
    psum x1, waiting for transfers between devices, reduce_attention(): lax.psum(shares[1].astype(jnp.bfloat16), 'narrow').astype(jnp.float32)  57.6 us
    reduce_scatter x1, waiting for transfers between devices, reduce_feedforward(): lax.psum_scatter(gradients[1].astype(jnp.bfloat16), 'wide', scatter_dimen...  50.7 us
    dot_general x1, matrix products, per_device(): jnp.dot(normed_two_low, full_up, preferred_element_type=jnp.float32)  38.1 us
    reduce_sum x3, other arithmetic, layer_norm(): return center * lax.rsqrt(spread + 1e-06) * gain + shift  31.2 us
    dot_general x12, matrix products, masked_scores(): jnp.einsum('qhd,khd->hqk', queries, key_rows, preferred_element_type=jnp....  31 us
    dot_general x6, matrix products, pair_forward(): jnp.einsum('hqk,khd->qhd', probabilities.astype(jnp.bfloat16), values, pr...  26.4 us
    dot_general x6, matrix products, pair_backward(): jnp.einsum('qhd,khd->hqk', grad_out, values, preferred_element_type=jnp.f...  25.1 us
  transfers between devices with their start and end apart: 10, of which 4 were waited for; matrix products, arithmetic and copies ran while one was open for 41% of the time, Pallas kernels for 0%

profile of v1, /device:TPU:0, one launch (start us, length us, event | category | flops | bytes accessed | tf_op | source)
XLA Modules:
  0.0 713.3 jit_solution(12938708907230480839)
XLA Ops:
  12.9 13.1 %fusion.92 = f32[1024]{0:T(1024)S(1)} fusion(f32[768]{0:T(1024)S(1)} %fusion.71, f32[1024]{0:T(1024)S(1)} %get-tuple-element.253, f32[1024]{0:T(1024)S(1)} %get-tuple-element.252, pred[768]{0:T(1024)(128)(4,1)S(1)} %get-tuple-element.266, f32[1024]{0:T(1024)S(1)} %fusion.76, pred[768]{0:T(1024)(128)(4,1)S(1)} %fusion.81, ...), kind=kLoop, calls=%fused_computation.165 | loop fusion | flops 5504000 | bytes 1594624 | tf_op jit(solution)/shard_map/reduce_sum | solution.py:20
  26.0 13.3 %multiply_reduce_fusion.6 = f32[1024]{0:T(1024)S(1)} fusion(f32[1024]{0:T(1024)S(1)} %broadcast_multiply_fusion.1, f32[768]{0:T(1024)S(1)} %fusion.71, f32[1024]{0:T(1024)S(1)} %get-tuple-element.253, f32[1024]{0:T(1024)S(1)} %get-tuple-element.252, pred[768]{0:T(1024)(128)(4,1)S(1)} %get-tuple-element.266, f32[1024]{0:T(1024)S(1)} %fusion.76, ...), kind=kLoop, calls=%fused_computation.97 | loop fusion | flops 7076864 | bytes 1598720 | tf_op jit(solution)/shard_map/reduce_sum | solution.py:21
  42.3 30.8 %all-reduce.18 = (bf16[768]{0:T(1024)(128)(2,1)S(1)}, bf16[768]{0:T(1024)(128)(2,1)S(1)}, bf16[768]{0:T(1024)(128)(2,1)S(1)}, bf16[768]{0:T(1024)(128)(2,1)S(1)}...) all-reduce(bf16[768]{0:T(1024)(128)(2,1)S(1)} %dynamic-update-slice, ...), channel_id=1, replica_groups=mesh['narrow'=4,'wide'=8] {'wide'}, use_global_device_ids=true, to_apply=%add.3 | all-reduce | flops 5376 | bytes 21504
  73.2 12.8 %all-gather.1 = bf16[8,1,384]{2,1,0:T(2,128)(2,1)S(1)} all-gather(bf16[1,1,384]{2,1,0:T(2,128)(2,1)S(1)} %reshape.409), channel_id=1, replica_groups=mesh['narrow'=4,'wide'=8] {'wide'}, dimensions={0}, use_global_device_ids=true | all-gather | bytes 6912 | tf_op jit(solution)/shard_map/all_gather | solution.py:244
  87.7 14.2 %add_convert_fusion.13 = bf16[1024,768]{0,1:T(8,128)(2,1)} fusion(f32[768]{0:T(1024)S(1)} %convert_element_type.210, f32[768]{0:T(1024)S(1)} %convert_element_type.209, f32[1024]{0:T(1024)S(1)} %fusion.86, f32[1024]{0:T(1024)S(1)} %broadcast_multiply_fusion.1, f32[768]{0:T(1024)S(1)} %fusion.71, f32[1024]{0:T(1024)S(1)} %get-tuple-element.253, ...), kind=kLoop, calls=%fused_computation.96.clone.clone.2 | loop fusion | flops 8650752 | bytes 3177728 | tf_op jit(solution)/shard_map/rd,re->de/dot_general | solution.py:324
  101.9 17.8 %add_convert_fusion.1 = bf16[1024,2304]{1,0:T(8,128)(2,1)S(1)} fusion(bf16[768,2304]{1,0:T(8,128)(2,1)} %all-gather.8.cloned.1.call-done, f32[2304]{0:T(1024)S(1)} %pad_maximum_fusion.3, f32[768]{0:T(1024)S(1)} %convert_element_type.210, f32[768]{0:T(1024)S(1)} %convert_element_type.209, f32[1024]{0:T(1024)S(1)} %fusion.86, ...), kind=kOutput, calls=%fused_computation.79 | convolution fusion | flops 3637248000 | bytes 9871616 | tf_op jit(solution)/shard_map/dot_general | solution.py:222
  129.0 59.7 %while.26 = (s32[]{:T(128)}, bf16[6,1024,2,64]{1,3,2,0:T(8,128)(2,1)}, f32[6,2,1024]{2,1,0:T(2,128)S(1)}, bf16[6,1024,2,64]{1,3,2,0:T(8,128)(2,1)}, s32[6,1024]{...) while((s32[]{:T(128)}, ...), condition=%wide.region_6.7_spmd, body=%wide.region_3.6_spmd.sunk | while | flops 563083264 | bytes 30750812 | solution.py:230
  129.7 2.8 fusion.141
  134.5 4.4 fusion.143
  139.6 2.8 fusion.141
  144.5 4.4 fusion.143
  149.6 2.8 fusion.141
  154.4 4.4 fusion.143
  159.5 2.9 fusion.141
  164.4 4.4 fusion.143
  169.5 2.8 fusion.141
  174.3 4.4 fusion.143
  179.4 2.8 fusion.141
  184.3 4.4 fusion.143
  188.8 15.3 %fusion.99 = (f32[1024]{0:T(1024)S(1)}, f32[1024,768]{0,1:T(8,128)S(1)}) fusion(f32[768]{0:T(1024)S(1)} %convert_element_type.219, bf16[1024,768]{0,1:T(8,128)(2,1)} %bitcast.32, bf16[768,768]{1,0:T(8,128)(2,1)} %all-gather.10.cloned.1.call-done, f32[768]{0:T(1024)S(1)} %fusion.71, f32[1024]{0:T(1024)S(1)} %get-tuple-element.253, ...), kind=kOutput, calls=%fused_computation.170 | convolution fusion | flops 1215036416 | bytes 7495936 | tf_op jit(solution)/shard_map/dot_general | solution.py:236
  206.2 38.1 %multiply_convert_fusion.1 = (bf16[1024,3072]{1,0:T(8,128)(2,1)}, f32[1024,3072]{1,0:T(8,128)}, f32[1024,3072]{1,0:T(8,128)}) fusion(f32[3072]{0:T(1024)S(1)} %bitcast.184, bf16[768,3072]{1,0:T(8,128)(2,1)} %all-gather.12.cloned.1.call-done, f32[1024,768]{0,1:T(8,128)} %copy-done.2, f32[768]{0:T(1024)S(1)} %convert_element_type.221, ...), kind=kOutput, calls=%fused_computation.65 | convolution fusion | flops 5043388416 | bytes 39348224 | tf_op jit(solution)/shard_map/dot_general | solution.py:251
  244.3 17.4 %fusion.102 = (bf16[3072]{0:T(1024)(128)(2,1)}, bf16[1024,3072]{1,0:T(8,128)(2,1)}) fusion(f32[1024,3072]{1,0:T(8,128)} %get-tuple-element.244, bf16[1024,768]{1,0:T(8,128)(2,1)S(1)} %copy-done.10, bf16[3072,768]{1,0:T(8,128)(2,1)} %all-gather.14.cloned.1.call-done, f32[1024,3072]{1,0:T(8,128)} %get-tuple-element.258, f32[3072]{0:T(1024)S(1)} %bitcast.185), kind=kOutput, calls=%fused_computation.173 | convolution fusion | flops 4882166784 | bytes 37767168 | tf_op jit(solution)/shard_map/rd,fd->rf/dot_general | solution.py:271
  261.7 10.7 %fusion.101 = (bf16[768]{0:T(1024)(128)(2,1)}, f32[1024,768]{1,0:T(8,128)}) fusion(bf16[1024,3072]{1,0:T(8,128)(2,1)} %get-tuple-element.264, bf16[768,3072]{1,0:T(8,128)(2,1)} %all-gather.12.cloned.1.call-done), kind=kOutput, calls=%fused_computation.172 | convolution fusion | flops 4832623616 | bytes 14157312 | tf_op jit(solution)/shard_map/rf,df->rd/dot_general | solution.py:278
  272.4 3.7 copy.91
  276.0 3.5 multiply_reduce_fusion.1
  289.6 121.9 %while.27 = (s32[]{:T(128)}, bf16[6,1024,2,64]{1,3,2,0:T(8,128)(2,1)}, bf16[6,1024,2,64]{1,3,2,0:T(8,128)(2,1)}, bf16[6,1024,2,64]{1,3,2,0:T(8,128)(2,1)}, bf16[...) while((s32[]{:T(128)}, ...), condition=%wide.region_13.14_spmd, body=%wide.region_11.13_spmd.sunk | while | flops 1374943232 | bytes 83174576 | solution.py:311
  292.6 4.2 multiply_reduce_fusion.8
  296.8 2.7 multiply_convert_fusion.3
  299.5 3.2 fusion.154
  305.7 4.2 fusion.155
  312.9 4.2 multiply_reduce_fusion.8
  317.1 2.7 multiply_convert_fusion.3
  319.8 3.2 fusion.154
  326.1 4.2 fusion.155
  333.3 4.2 multiply_reduce_fusion.8
  337.5 2.7 multiply_convert_fusion.3
  340.2 3.2 fusion.154
  346.4 4.2 fusion.155
  353.6 4.2 multiply_reduce_fusion.8
  357.8 2.7 multiply_convert_fusion.3
  360.5 3.1 fusion.154
  366.7 4.2 fusion.155
  373.9 4.2 multiply_reduce_fusion.8
  380.8 3.2 fusion.154
  387.0 4.2 fusion.155
  394.2 4.2 multiply_reduce_fusion.8
  401.1 3.2 fusion.154
  407.3 4.1 fusion.155
  411.5 8.4 %convolution_convert_fusion.2 = bf16[768,2304]{1,0:T(8,128)(2,1)} fusion(bf16[1024,768]{0,1:T(8,128)(2,1)} %bitcast.51, bf16[1024,768]{0,1:T(8,128)(2,1)} %bitcast.179, bf16[1024,768]{0,1:T(8,128)(2,1)} %bitcast.175, bf16[1024,768]{0,1:T(8,128)(2,1)} %add_convert_fusion.13), kind=kOutput, calls=%fused_computation.82 | convolution fusion | flops 3639803904 | bytes 9830400 | tf_op jit(solution)/shard_map/rd,re->de/dot_general | solution.py:324
  420.2 4.3 convolution_convert_fusion.4
  424.6 9.8 %convolution_convert_fusion.1 = bf16[768,3072]{1,0:T(8,128)(2,1)} fusion(bf16[1024,3072]{1,0:T(8,128)(2,1)} %get-tuple-element.264, f32[1024,768]{0,1:T(8,128)S(1)} %copy-done.3, f32[768]{0:T(1024)S(1)} %copy-done.47, f32[768]{0:T(1024)S(1)} %convert_element_type.220, f32[1024]{0:T(1024)S(1)} %fusion.87, f32[1024]{0:T(1024)S(1)} %broadcast_multiply_fusion), kind=kOutput, calls=%fused_computation.81 | convolution fusion | flops 4838129664 | bytes 14170112 | tf_op jit(solution)/shard_map/rd,rf->df/dot_general | solution.py:275
  435.8 9.8 %convolution_convert_fusion = bf16[3072,768]{1,0:T(8,128)(2,1)} fusion(bf16[1024,3072]{1,0:T(8,128)(2,1)} %get-tuple-element.243, bf16[1024,768]{1,0:T(8,128)(2,1)S(1)} %copy-done.11), kind=kOutput, calls=%fused_computation.80 | convolution fusion | flops 4834197504 | bytes 12582912 | tf_op jit(solution)/shard_map/rf,rd->fd/dot_general | solution.py:268
  447.7 8.7 %fusion.100 = (bf16[768]{0:T(1024)(128)(2,1)S(1)}, f32[1024,768]{1,0:T(8,128)}) fusion(bf16[768,2304]{1,0:T(8,128)(2,1)} %all-gather.8.cloned.1.call-done, bf16[1024,768]{0,1:T(8,128)(2,1)} %bitcast.51, bf16[1024,768]{0,1:T(8,128)(2,1)} %bitcast.180, bf16[1024,768]{0,1:T(8,128)(2,1)S(1)} %bitcast.176), kind=kOutput, calls=%fused_computation.171 | convolution fusion | flops 3638820096 | bytes 11404800 | tf_op jit(solution)/shard_map/re,de->rd/dot_general | solution.py:327
  456.4 5.9 reduce-scatter.5.cloned.1.call-done
  467.3 14.3 %multiply_reduce_fusion.3 = f32[1024]{0:T(1024)S(1)} fusion(f32[1024,768]{0,1:T(8,128)S(1)} %copy.92, f32[768]{0:T(1024)S(1)} %copy-done.28, f32[1024]{0:T(1024)S(1)} %copy-done.26, f32[768]{0:T(1024)S(1)} %copy-done.18, f32[1024]{0:T(1024)S(1)} %copy-done.22, f32[1024]{0:T(1024)S(1)} %copy-done.20, pred[768]{0:T(1024)(128)(4,1)S(1)} %copy-done.36, ...), kind=kLoop, calls=%fused_computation.89 | loop fusion | flops 7863296 | bytes 4747520 | tf_op jit(solution)/shard_map/transpose(jvp())/reduce_sum | solution.py:22
  481.6 13.4 %multiply_reduce_fusion.2 = (bf16[768]{0:T(1024)(128)(2,1)S(1)}, f32[1024]{0:T(1024)S(1)}) fusion(f32[1024,768]{0,1:T(8,128)S(1)} %copy.92, f32[1024]{0:T(1024)S(1)} %copy-done.30, f32[1024]{0:T(1024)S(1)} %copy-done.26, f32[768]{0:T(1024)S(1)} %copy-done.18, f32[1024]{0:T(1024)S(1)} %copy-done.22, f32[1024]{0:T(1024)S(1)} %copy-done.20, ...), kind=kLoop, calls=%fused_computation.87 | loop fusion | flops 12581120 | bytes 4757248 | tf_op jit(solution)/shard_map/transpose(jvp())/reduce_sum | solution.py:22
  495.1 27.8 %all-reduce.17 = (bf16[768]{0:T(1024)(128)(2,1)S(1)}, bf16[768]{0:T(1024)(128)(2,1)S(1)}, bf16[768]{0:T(1024)(128)(2,1)S(1)}, bf16[768]{0:T(1024)(128)(2,1)S(1)}...) all-reduce(bf16[768]{0:T(1024)(128)(2,1)S(1)} %dynamic-update-slice, ...), channel_id=1, replica_groups=mesh['narrow'=4,'wide'=8] {'wide'}, use_global_device_ids=true, to_apply=%add.7 | all-reduce | flops 9984 | bytes 39936
  523.5 10.0 %all-reduce.19 = (bf16[96]{0:T(256)(128)(2,1)S(1)}, bf16[96]{0:T(256)(128)(2,1)S(1)}, bf16[96]{0:T(256)(128)(2,1)S(1)}, bf16[96]{0:T(256)(128)(2,1)S(1)}, bf16[9...) all-reduce(bf16[96]{0:T(256)(128)(2,1)S(1)} %dynamic-slice.9, ...), channel_id=1, replica_groups=mesh['narrow'=4,'wide'=8] {'narrow'}, use_global_device_ids=true, to_apply=%region_26.27 | all-reduce | flops 1152 | bytes 4608 | tf_op jit(solution)/shard_map/psum | solution.py:159
  538.2 16.3 %add_convert_fusion.2 = bf16[1024,768]{0,1:T(8,128)(2,1)} fusion(f32[1024,768]{0,1:T(8,128)} %copy-done.6, bf16[1024,768]{0,1:T(8,128)(2,1)} %copy.90, f32[1024]{0:T(1024)S(1)} %negate_multiply_fusion.1, f32[1024]{0:T(1024)S(1)} %copy-done.32, f32[1024]{0:T(1024)S(1)} %multiply_multiply_fusion.5, f32[1024]{0:T(1024)S(1)} %copy-done.26, ...), kind=kLoop, calls=%fused_computation.88 | loop fusion | flops 14155776 | bytes 11051264 | tf_op jit(solution)/shard_map/convert_element_type | solution.py:333
  554.5 2.7 copy.96
  557.2 50.7 %reduce-scatter.11.cloned.1.call-done = bf16[384,768]{1,0:T(8,128)(2,1)} async-done(((bf16[3072,768]{1,0:T(8,128)(2,1)}), bf16[384,768]{1,0:T(8,128)(2,1)}) %reduce-scatter.11.cloned.1.call-update) | async-done | bytes 589840 | tf_op jit(solution)/shard_map/reduce_scatter | solution.py:106
  608.0 9.5 %add_convert_fusion.3 = bf16[1024,768]{0,1:T(8,128)(2,1)} fusion(f32[1024,768]{0,1:T(8,128)S(1)} %copy-done.4, bf16[1024,3072]{1,0:T(8,128)(2,1)} %get-tuple-element.243, bf16[3072,768]{1,0:T(8,128)(2,1)} %all-gather.14.cloned.1.call-done, f32[768]{0:T(1024)S(1)} %convert_element_type.225), kind=kOutput, calls=%fused_computation.92 | convolution fusion | flops 4834197504 | bytes 15731712 | tf_op jit(solution)/shard_map/dot_general | solution.py:258
  620.1 20.7 %all-gather.16.cloned.1.call-done = bf16[384,2304]{1,0:T(8,128)(2,1)} async-done(((bf16[96,2304]{1,0:T(8,128)(2,1)}), bf16[384,2304]{1,0:T(8,128)(2,1)}) %all-gather.16.cloned.1.call-update) | async-done | bytes 1769488 | tf_op jit(solution)/shard_map/all_gather | solution.py:15
  643.6 57.6 %all-reduce.23.cloned.1.call-done = (bf16[96,768]{1,0:T(8,128)(2,1)}, bf16[96,3072]{1,0:T(8,128)(2,1)}, bf16[384,768]{1,0:T(8,128)(2,1)}) async-done(((bf16[96,768]{1,0:T(8,128)(2,1)}, bf16[96,3072]{1,0:T(8,128)(2,1)}, bf16[384,768]{1,0:T(8,128)(2,1)}), (bf16[96,768]{1,0:T(8,128)(2,1)}, bf16[96,3072]{1,0:T(8,128)(2,1)}, bf16[384,768]{1,0:T(8,128)(2,1)})) %all-reduce.23.cloned.1.call-update) | async-done | bytes 1327120 | tf_op jit(solution)/shard_map/psum | solution.py:158
  (313 shorter events, 111.5 us)
Async XLA Ops:
  7.2 5.7 copy-start.37
  7.2 5.6 copy-start.51
  7.2 5.6 copy-start.38
  7.2 94.7 %all-gather.8.cloned.1.call-start = ((), (), s32[]{:S(2)}) async-start(), calls=%async_computation.4 | async-start | bytes 3981312 | tf_op jit(solution)/shard_map/all_gather | solution.py:205
  7.9 180.8 %all-gather.10.cloned.1.call-start = ((), (), s32[]{:S(2)}) async-start(), calls=%async_computation.5 | async-start | bytes 1327104 | tf_op jit(solution)/shard_map/all_gather | solution.py:206
  8.7 197.5 %all-gather.12.cloned.1.call-start = ((), (), s32[]{:S(2)}) async-start(), calls=%async_computation.6 | async-start | bytes 5308416 | tf_op jit(solution)/shard_map/all_gather | solution.py:240
  9.4 234.8 %all-gather.14.cloned.1.call-start = ((), (), s32[]{:S(2)}) async-start(), calls=%async_computation.7 | async-start | bytes 5308416 | tf_op jit(solution)/shard_map/all_gather | solution.py:241
  10.0 452.2 %reduce-scatter.5.cloned.1.call-start = ((), (), s32[]{:S(2)}) async-start(), calls=%async_computation.8 | async-start | bytes 3981312 | tf_op jit(solution)/shard_map/reduce_scatter | solution.py:134
  10.1 178.6 %copy-start.33 = (pred[768]{0:T(1024)(128)(4,1)}, pred[768]{0:T(1024)(128)(4,1)S(1)}, u32[]{:S(2)}) copy-start(pred[768]{0:T(1024)(128)(4,1)S(1)} %get-tuple-element.265) | copy-start | bytes 2308
  10.1 178.6 %copy-start.35 = (pred[768]{0:T(1024)(128)(4,1)}, pred[768]{0:T(1024)(128)(4,1)S(1)}, u32[]{:S(2)}) copy-start(pred[768]{0:T(1024)(128)(4,1)S(1)} %get-tuple-element.266) | copy-start | bytes 2308
  10.1 178.6 %copy-start.17 = (f32[768]{0:T(1024)}, f32[768]{0:T(1024)S(1)}, u32[]{:S(2)}) copy-start(f32[768]{0:T(1024)S(1)} %fusion.71) | copy-start | bytes 9220
  10.1 178.6 %copy-start.41 = (pred[768]{0:T(1024)(128)(4,1)}, pred[768]{0:T(1024)(128)(4,1)S(1)}, u32[]{:S(2)}) copy-start(pred[768]{0:T(1024)(128)(4,1)S(1)} %fusion.81) | copy-start | bytes 2308
  10.9 177.9 %copy-start.19 = (f32[1024]{0:T(1024)}, f32[1024]{0:T(1024)S(1)}, u32[]{:S(2)}) copy-start(f32[1024]{0:T(1024)S(1)} %get-tuple-element.252) | copy-start | bytes 12292
  10.9 177.9 %copy-start.21 = (f32[1024]{0:T(1024)}, f32[1024]{0:T(1024)S(1)}, u32[]{:S(2)}) copy-start(f32[1024]{0:T(1024)S(1)} %get-tuple-element.253) | copy-start | bytes 12292
  12.6 176.1 %copy-start = (bf16[1024,768]{0,1:T(8,128)(2,1)}, bf16[1024,768]{0,1:T(8,128)(2,1)S(1)}, u32[]{:S(2)}) copy-start(bf16[1024,768]{0,1:T(8,128)(2,1)S(1)} %copy.85) | copy-start | bytes 4718596
  12.6 26.7 %copy-start.49 = (u32[32]{0:T(128)S(1)}, u32[32]{0:T(128)}, u32[]{:S(2)}) copy-start(u32[32]{0:T(128)} %constant.212) | copy-start | bytes 388
  12.7 28.0 %copy-start.53 = (bf16[96]{0:T(256)(128)(2,1)S(1)}, bf16[96]{0:T(256)(128)(2,1)}, u32[]{:S(2)}) copy-start(bf16[96]{0:T(256)(128)(2,1)} %param.31) | copy-start | bytes 580
  12.7 28.2 %copy-start.54 = (bf16[96]{0:T(256)(128)(2,1)S(1)}, bf16[96]{0:T(256)(128)(2,1)}, u32[]{:S(2)}) copy-start(bf16[96]{0:T(256)(128)(2,1)} %param.32) | copy-start | bytes 580
  12.7 28.4 %copy-start.55 = (bf16[96]{0:T(256)(128)(2,1)S(1)}, bf16[96]{0:T(256)(128)(2,1)}, u32[]{:S(2)}) copy-start(bf16[96]{0:T(256)(128)(2,1)} %param.33) | copy-start | bytes 580
  12.7 28.6 %copy-start.56 = (bf16[96]{0:T(256)(128)(2,1)S(1)}, bf16[96]{0:T(256)(128)(2,1)}, u32[]{:S(2)}) copy-start(bf16[96]{0:T(256)(128)(2,1)} %param.34) | copy-start | bytes 580
  12.7 28.9 %copy-start.57 = (bf16[96]{0:T(256)(128)(2,1)S(1)}, bf16[96]{0:T(256)(128)(2,1)}, u32[]{:S(2)}) copy-start(bf16[96]{0:T(256)(128)(2,1)} %param.35) | copy-start | bytes 580
  12.7 29.1 %copy-start.58 = (bf16[96]{0:T(256)(128)(2,1)S(1)}, bf16[96]{0:T(256)(128)(2,1)}, u32[]{:S(2)}) copy-start(bf16[96]{0:T(256)(128)(2,1)} %param.36) | copy-start | bytes 580
  12.7 29.3 %copy-start.59 = (bf16[96]{0:T(256)(128)(2,1)S(1)}, bf16[96]{0:T(256)(128)(2,1)}, u32[]{:S(2)}) copy-start(bf16[96]{0:T(256)(128)(2,1)} %param.37) | copy-start | bytes 580
  12.7 60.4 %copy-start.50 = (bf16[384]{0:T(512)(128)(2,1)S(1)}, bf16[384]{0:T(512)(128)(2,1)}, u32[]{:S(2)}) copy-start(bf16[384]{0:T(512)(128)(2,1)} %param.38) | copy-start | bytes 2308
  12.8 73.2 %copy-start.9 = (bf16[1024,768]{1,0:T(8,128)(2,1)S(1)}, bf16[1024,768]{1,0:T(8,128)(2,1)}, u32[]{:S(2)}) copy-start(bf16[1024,768]{1,0:T(8,128)(2,1)} %param.26) | copy-start | bytes 4718596
  12.9 175.9 %copy-start.23 = (f32[1024]{0:T(1024)}, f32[1024]{0:T(1024)S(1)}, u32[]{:S(2)}) copy-start(f32[1024]{0:T(1024)S(1)} %fusion.76) | copy-start | bytes 12292
  26.0 75.9 %copy-start.25 = (f32[1024]{0:T(1024)}, f32[1024]{0:T(1024)S(1)}, u32[]{:S(2)}) copy-start(f32[1024]{0:T(1024)S(1)} %broadcast_multiply_fusion.1) | copy-start | bytes 12292
  39.3 33.8 %copy-start.39 = (f32[1024]{0:T(1024)}, f32[1024]{0:T(1024)S(1)}, u32[]{:S(2)}) copy-start(f32[1024]{0:T(1024)S(1)} %multiply_reduce_fusion.6) | copy-start | bytes 12292
  39.3 62.6 %copy-start.29 = (f32[1024]{0:T(1024)}, f32[1024]{0:T(1024)S(1)}, u32[]{:S(2)}) copy-start(f32[1024]{0:T(1024)S(1)} %fusion.86) | copy-start | bytes 12292
  73.1 28.8 %copy-start.27 = (f32[768]{0:T(1024)}, f32[768]{0:T(1024)S(1)}, u32[]{:S(2)}) copy-start(f32[768]{0:T(1024)S(1)} %convert_element_type.209) | copy-start | bytes 9220
  73.2 133.0 %copy-start.46 = (f32[768]{0:T(1024)}, f32[768]{0:T(1024)S(1)}, u32[]{:S(2)}) copy-start(f32[768]{0:T(1024)S(1)} %convert_element_type.221) | copy-start | bytes 9220
  188.7 15.3 %copy-start.8 = (bf16[6,1024,2,64]{1,3,2,0:T(8,128)(2,1)}, bf16[6,1024,2,64]{1,3,2,0:T(8,128)(2,1)S(1)}, u32[]{:S(2)}) copy-start(bf16[6,1024,2,64]{1,3,2,0:T(8,128)(2,1)S(1)} %get-tuple-element.451) | copy-start | bytes 4718596
  206.2 38.1 %copy-start.10 = (bf16[1024,768]{1,0:T(8,128)(2,1)S(1)}, bf16[1024,768]{1,0:T(8,128)(2,1)}, u32[]{:S(2)}) copy-start(bf16[1024,768]{1,0:T(8,128)(2,1)} %param.26) | copy-start | bytes 4718596
  272.4 3.7 copy-start.3
  276.0 3.5 copy-start.5
  282.1 3.3 copy-start.15
  299.5 3.2 copy-start.12
  380.8 3.2 copy-start.12
  401.1 3.2 copy-start.12
  419.9 4.6 copy-start.47
  420.0 137.3 %reduce-scatter.7.cloned.1.call-start = ((), (), s32[]{:S(2)}) async-start(), calls=%async_computation.9 | async-start | bytes 1327104 | tf_op jit(solution)/shard_map/reduce_scatter | solution.py:137
  424.5 132.7 %reduce-scatter.9.cloned.1.call-start = ((), (), s32[]{:S(2)}) async-start(), calls=%async_computation.10 | async-start | bytes 5308416 | tf_op jit(solution)/shard_map/reduce_scatter | solution.py:103
  434.4 173.6 %reduce-scatter.11.cloned.1.call-start = ((), (), s32[]{:S(2)}) async-start(), calls=%async_computation.11 | async-start | bytes 5308416 | tf_op jit(solution)/shard_map/reduce_scatter | solution.py:106
  445.7 195.1 %all-gather.16.cloned.1.call-start = ((), (), s32[]{:S(2)}) async-start(), calls=%async_computation.12 | async-start | bytes 2211840 | tf_op jit(solution)/shard_map/all_gather | solution.py:15
  462.3 238.9 %all-reduce.23.cloned.1.call-start = ((), (), s32[]{:S(2)}) async-start(), calls=%async_computation.13 | async-start | bytes 2654208 | tf_op jit(solution)/shard_map/psum | solution.py:158
  462.8 4.4 copy-start.18
  462.8 4.4 copy-start.20
  462.8 4.3 copy-start.22
  462.8 4.3 copy-start.24
  462.9 4.3 copy-start.26
  462.9 4.3 copy-start.28
  462.9 4.3 copy-start.34
  462.9 4.3 copy-start.36
  462.9 4.3 copy-start.42
  465.4 16.2 %copy-start.40 = (f32[1024]{0:T(1024)S(1)}, f32[1024]{0:T(1024)}, u32[]{:S(2)}) copy-start(f32[1024]{0:T(1024)} %copy-done.39) | copy-start | bytes 12292
  465.4 16.2 %copy-start.30 = (f32[1024]{0:T(1024)S(1)}, f32[1024]{0:T(1024)}, u32[]{:S(2)}) copy-start(f32[1024]{0:T(1024)} %copy-done.29) | copy-start | bytes 12292
  467.2 14.4 %copy-start.1 = (bf16[1024,768]{0,1:T(8,128)(2,1)S(1)}, bf16[1024,768]{0,1:T(8,128)(2,1)}, u32[]{:S(2)}) copy-start(bf16[1024,768]{0,1:T(8,128)(2,1)} %copy-done) | copy-start | bytes 4718596
  481.5 13.5 %copy-start.43 = (bf16[768]{0:T(1024)(128)(2,1)S(1)}, bf16[768]{0:T(1024)(128)(2,1)}, u32[]{:S(2)}) copy-start(bf16[768]{0:T(1024)(128)(2,1)} %get-tuple-element.239) | copy-start | bytes 4612
  481.6 13.5 %copy-start.44 = (bf16[768]{0:T(1024)(128)(2,1)S(1)}, bf16[768]{0:T(1024)(128)(2,1)}, u32[]{:S(2)}) copy-start(bf16[768]{0:T(1024)(128)(2,1)} %get-tuple-element.172) | copy-start | bytes 4612
  481.6 13.5 %copy-start.45 = (bf16[3072]{0:T(1024)(128)(2,1)S(1)}, bf16[3072]{0:T(1024)(128)(2,1)}, u32[]{:S(2)}) copy-start(bf16[3072]{0:T(1024)(128)(2,1)} %get-tuple-element.263) | copy-start | bytes 18436
  481.6 13.5 %copy-start.48 = (bf16[768]{0:T(1024)(128)(2,1)S(1)}, bf16[768]{0:T(1024)(128)(2,1)}, u32[]{:S(2)}) copy-start(bf16[768]{0:T(1024)(128)(2,1)} %get-tuple-element.261) | copy-start | bytes 4612
  481.6 56.6 %copy-start.32 = (f32[1024]{0:T(1024)S(1)}, f32[1024]{0:T(1024)}, u32[]{:S(2)}) copy-start(f32[1024]{0:T(1024)} %copy-done.31) | copy-start | bytes 12292
  554.5 53.5 %copy-start.4 = (f32[1024,768]{0,1:T(8,128)S(1)}, f32[1024,768]{0,1:T(8,128)}, u32[]{:S(2)}) copy-start(f32[1024,768]{0,1:T(8,128)} %copy-done.2) | copy-start | bytes 9437188
  701.2 4.4 copy-start.16
  (17 other events, 30.5 us)
Sparse Core Ops, SparseCore 0:
  9.7 44.2 all-gather.7
  55.6 21.6 all-gather.9
  78.9 50.9 all-gather.11
  131.4 49.9 all-gather.13
  420.1 42.1 reduce-scatter.4
  465.0 31.5 reduce-scatter.6
  498.9 53.3 reduce-scatter.8
  554.6 53.3 reduce-scatter.10
  609.8 30.9 all-gather.15
  644.0 57.0 all-reduce.22
